TPU v7x, 32 devices: a whole 2x2x4 slice. The times are simulated.
32 devices in a mesh: dp: 16 (over z, x, core), tensor: 2 (over y).
Axes of the slice: x: 2, y: 2, z: 4, core: 2. Of those that a mesh axis runs over, the one named last changes fastest.
Arguments:
- inputs: bfloat16 [16384, 768], P(('dp', 'tensor')), may hold values from -6 to 6
- teacher: bfloat16 [16384, 768], P(('dp', 'tensor')), may hold values from -6 to 6
- lengths: int32 [16], P('dp'), may hold values from 256 to 1024
- w_query: bfloat16 [768, 768], P(('tensor', 'dp')), may hold values from -0.3125 to 0.3125
- w_key: bfloat16 [768, 768], P(('tensor', 'dp')), may hold values from -0.3125 to 0.3125
- w_value: bfloat16 [768, 768], P(('tensor', 'dp')), may hold values from -0.21875 to 0.21875
- w_out: bfloat16 [768, 768], P(('tensor', 'dp')), may hold values from -1.25 to 1.25
- w_up: bfloat16 [3072, 768], P(('tensor', 'dp')), may hold values from -0.21875 to 0.21875
- w_down: bfloat16 [3072, 768], P(('tensor', 'dp')), may hold values from -0.21875 to 0.21875
- b_query: float32 [768], replicated, may hold values from -3 to 3
- b_value: float32 [768], replicated, may hold values from -1.25 to 1.25
- b_out: float32 [768], replicated, may hold values from -1.75 to 1.75
- b_up: float32 [3072], replicated, may hold values from -3 to 3
- b_down: float32 [768], replicated, may hold values from -1.75 to 1.75
- gain_one: float32 [768], replicated, may hold values from 0.5 to 1.5
- shift_one: float32 [768], replicated, may hold values from -1.75 to 1.75
- gain_two: float32 [768], replicated, may hold values from 0.5 to 1.5
- shift_two: float32 [768], replicated, may hold values from -1.75 to 1.75
- z_head: float32 [12], replicated, may hold values from 0.4 to 1
- z_mha: float32 [1], replicated, may hold values from 0.4 to 1
- z_hidden: float32 [768], replicated, may hold values from 0.4 to 1
- z_int: float32 [3072], replicated, may hold values from 0.4 to 1
- z_ffn: float32 [1], replicated, may hold values from 0.4 to 1
Outputs:
- layer_out: float32 [16384, 768], P(('dp', 'tensor'))
- loss_value: float32 [1], replicated
- grad_inputs: float32 [16384, 768], P(('dp', 'tensor'))
- grad_w_query: float32 [768, 768], P(('tensor', 'dp'))
- grad_w_key: float32 [768, 768], P(('tensor', 'dp'))
- grad_w_value: float32 [768, 768], P(('tensor', 'dp'))
- grad_w_out: float32 [768, 768], P(('tensor', 'dp'))
- grad_w_up: float32 [3072, 768], P(('tensor', 'dp'))
- grad_w_down: float32 [3072, 768], P(('tensor', 'dp'))
- grad_b_query: float32 [768], replicated
- grad_b_value: float32 [768], replicated
- grad_b_out: float32 [768], replicated
- grad_b_up: float32 [3072], replicated
- grad_b_down: float32 [768], replicated
- grad_gain_one: float32 [768], replicated
- grad_shift_one: float32 [768], replicated
- grad_gain_two: float32 [768], replicated
- grad_shift_two: float32 [768], replicated
- grad_z_head: float32 [12], replicated
- grad_z_mha: float32 [1], replicated
- grad_z_hidden: float32 [768], replicated
- grad_z_int: float32 [3072], replicated
- grad_z_ffn: float32 [1], replicated
All inputs are finite; a program needn't handle non-finite values.
Results may differ from a plain program's by a relative error of at most 0.013.
The roundings to bfloat16 on the way count: a program that leaves them out, or rounds other values in their place, can miss the bound.
Values may be sent and summed in bfloat16 or wider, within the bound.
A program may use at most 192 MiB of HBM per device.

v0:
```python
import math
import jax
import jax.numpy as jnp
from jax import lax
from jax.sharding import PartitionSpec as P

D = 768
HEADS = 12
FF = 3072
SEQ = 1024
epsilon = 1e-12


def norm_rows(summed, gain_vec, shift_vec):
    average = jnp.mean(summed, axis=-1, keepdims=True)
    centered = summed - average
    variance = jnp.mean(centered * centered, axis=-1, keepdims=True)
    return centered * lax.rsqrt(variance + epsilon) * gain_vec + shift_vec


def gelu_exact(values):
    return jax.nn.gelu(values, approximate=False)


def times_plain(left, right):
    return jnp.dot(left, right, preferred_element_type=jnp.float32)


def times_trans(left, right):
    return lax.dot_general(
        left, right, (((1,), (1,)), ((), ())), preferred_element_type=jnp.float32
    )


def trans_times(left, right):
    return lax.dot_general(
        left, right, (((0,), (0,)), ((), ())), preferred_element_type=jnp.float32
    )


def gather_attn(w_query, w_key, w_value, w_out):
    return (
        lax.all_gather(w_query, "dp", axis=0, tiled=True),
        lax.all_gather(w_key, "dp", axis=0, tiled=True),
        lax.all_gather(w_value, "dp", axis=0, tiled=True),
        lax.all_gather(w_out, "dp", axis=0, tiled=True),
    )


def gather_ffn(w_up, w_down):
    return (
        lax.all_gather(w_up, "dp", axis=0, tiled=True),
        lax.all_gather(w_down, "dp", axis=0, tiled=True),
    )


def spread_into(local_vec, full_len, offset):
    return lax.dynamic_update_slice(jnp.zeros((full_len,), jnp.float32), local_vec, (offset,))


def on_device(
    inputs,
    teacher,
    lengths,
    w_query,
    w_key,
    w_value,
    w_out,
    w_up,
    w_down,
    b_query,
    b_value,
    b_out,
    b_up,
    b_down,
    gain_one,
    shift_one,
    gain_two,
    shift_two,
    z_head,
    z_mha,
    z_hidden,
    z_int,
    z_ffn,
):
    rows_own = inputs.shape[0]
    tensor_pos = lax.axis_index("tensor")
    tensor_count = lax.axis_size("tensor")
    group_rows = rows_own * tensor_count
    seq_count = group_rows // SEQ
    head_size = D // HEADS
    local_width = D // tensor_count
    heads_local = local_width // head_size
    units_local = FF // tensor_count
    qblock = min(512, SEQ)
    nblocks = SEQ // qblock
    softmax_scale = 1.0 / math.sqrt(head_size)
    positions = jnp.arange(group_rows, dtype=jnp.int32)
    seq_of_row = positions // SEQ
    picks = seq_of_row[:, None] == jnp.arange(seq_count, dtype=jnp.int32)[None, :]
    row_length = jnp.sum(jnp.where(picks, lengths[None, :], 0), axis=1)
    valid_group = positions % SEQ < row_length
    valid_own = lax.dynamic_slice_in_dim(valid_group, tensor_pos * rows_own, rows_own)
    head_start = tensor_pos * local_width
    unit_start = tensor_pos * units_local
    bias_query = lax.dynamic_slice_in_dim(b_query, head_start, local_width)
    bias_value = lax.dynamic_slice_in_dim(b_value, head_start, local_width)
    gate_heads = lax.dynamic_slice_in_dim(z_head, tensor_pos * heads_local, heads_local)
    bias_up = lax.dynamic_slice_in_dim(b_up, unit_start, units_local)
    gate_units = lax.dynamic_slice_in_dim(z_int, unit_start, units_local)
    wq_full, wk_full, wv_full, wo_full = gather_attn(w_query, w_key, w_value, w_out)
    x_group = lax.all_gather(inputs, "tensor", axis=0, tiled=True)
    query = ((times_trans(x_group, wq_full) + bias_query) * softmax_scale).astype(jnp.bfloat16)
    keys_b = times_trans(x_group, wk_full).astype(jnp.bfloat16)
    values_b = (times_trans(x_group, wv_full) + bias_value).astype(jnp.bfloat16)
    query5 = query.reshape(seq_count, nblocks, qblock, heads_local, head_size)
    keys4 = keys_b.reshape(seq_count, SEQ, heads_local, head_size)
    values4 = values_b.reshape(seq_count, SEQ, heads_local, head_size)
    valid2 = valid_group.reshape(seq_count, SEQ)

    def forward_seq(element):
        query_seq, keys_seq, values_seq, key_valid = element

        def forward_block(query_blk):
            scores = jnp.einsum(
                "qhd,khd->hqk", query_blk, keys_seq, preferred_element_type=jnp.float32
            )
            scores = jnp.where(key_valid[None, None, :], scores, -1e30)
            highest = jnp.max(scores, axis=-1, keepdims=True)
            exponent = jnp.exp(scores - highest)
            denominator = jnp.sum(exponent, axis=-1, keepdims=True)
            attention = (exponent / denominator).astype(jnp.bfloat16)
            context = jnp.einsum(
                "hqk,khd->qhd", attention, values_seq, preferred_element_type=jnp.float32
            )
            return (context, (highest + jnp.log(denominator))[..., 0])

        return lax.map(forward_block, query_seq)

    context_all, logsum_all = lax.map(forward_seq, (query5, keys4, values4, valid2))
    context_f = context_all.reshape(group_rows, heads_local, head_size)
    gated = (
        (context_f * gate_heads[None, :, None])
        .reshape(group_rows, local_width)
        .astype(jnp.bfloat16)
    )
    attn_out = (
        lax.psum_scatter(times_plain(gated, wo_full), "tensor", scatter_dimension=0, tiled=True)
        + b_out
    )
    branch_attn = z_mha * z_hidden
    first_sum = inputs.astype(jnp.float32) + branch_attn * attn_out
    first_norm = norm_rows(first_sum, gain_one, shift_one)
    y_group = lax.all_gather(first_norm.astype(jnp.bfloat16), "tensor", axis=0, tiled=True)
    wu_full, wd_full = gather_ffn(w_up, w_down)
    upper = times_trans(y_group, wu_full) + bias_up
    activated = gelu_exact(upper)
    hidden_b = (activated * gate_units).astype(jnp.bfloat16)
    down = (
        lax.psum_scatter(times_plain(hidden_b, wd_full), "tensor", scatter_dimension=0, tiled=True)
        + b_down
    )
    branch_ffn = z_ffn * z_hidden
    second_sum = first_norm + branch_ffn * down
    output = norm_rows(second_sum, gain_two, shift_two)
    residue = output - teacher.astype(jnp.float32)
    masked = jnp.where(valid_own[:, None], residue, 0.0)
    valid_count, square_sum = lax.psum(
        (jnp.sum(valid_own.astype(jnp.float32)), jnp.sum(masked * masked)), ("dp", "tensor")
    )
    loss_value = square_sum / (D * valid_count)
    tokens_all = group_rows * lax.axis_size("dp")
    grad_out = masked * (2.0 * tokens_all / valid_count)
    ffn_back = gather_ffn(w_up, w_down)
    attn_back = gather_attn(w_query, w_key, w_value, w_out)
    unused, pull_two = jax.vjp(norm_rows, second_sum, gain_two, shift_two)
    grad_second, grad_gain_two, grad_shift_two = pull_two(grad_out)
    grad_down = (grad_second * branch_ffn).astype(jnp.bfloat16)
    grad_z_ffn = jnp.sum(grad_second * z_hidden * down).reshape(1)
    hidden_part = jnp.sum(grad_second * z_ffn * down, axis=0)
    grad_b_down = jnp.sum(grad_down.astype(jnp.float32), axis=0)
    down_group = lax.all_gather(grad_down, "tensor", axis=0, tiled=True)
    grad_w_down = trans_times(hidden_b, down_group)
    grad_hidden = times_trans(down_group, ffn_back[1])
    grad_z_int_local = jnp.sum(grad_hidden * activated, axis=0)
    unused, gelu_pull = jax.vjp(gelu_exact, upper)
    grad_upper = gelu_pull(grad_hidden * gate_units)[0].astype(jnp.bfloat16)
    grad_b_up_local = jnp.sum(grad_upper.astype(jnp.float32), axis=0)
    grad_w_up = trans_times(grad_upper, y_group)
    grad_first_norm = grad_second + lax.psum_scatter(
        times_plain(grad_upper, ffn_back[0]), "tensor", scatter_dimension=0, tiled=True
    )
    unused, pull_one = jax.vjp(norm_rows, first_sum, gain_one, shift_one)
    grad_first, grad_gain_one, grad_shift_one = pull_one(grad_first_norm)
    grad_attn = (grad_first * branch_attn).astype(jnp.bfloat16)
    grad_z_mha = jnp.sum(grad_first * z_hidden * attn_out).reshape(1)
    hidden_part = hidden_part + jnp.sum(grad_first * z_mha * attn_out, axis=0)
    grad_b_out = jnp.sum(grad_attn.astype(jnp.float32), axis=0)
    attn_group = lax.all_gather(grad_attn, "tensor", axis=0, tiled=True)
    grad_w_out = trans_times(gated, attn_group)
    grad_gated = times_trans(attn_group, attn_back[3]).reshape(group_rows, heads_local, head_size)
    grad_z_head_local = jnp.sum(grad_gated * context_f, axis=(0, 2))
    grad_heads = (grad_gated * gate_heads[None, :, None]).astype(jnp.bfloat16)
    grad_heads5 = grad_heads.reshape(seq_count, nblocks, qblock, heads_local, head_size)

    def backward_seq(element):
        query_seq, keys_seq, values_seq, key_valid, grad_seq, logsum_seq = element
        initial = jnp.zeros((SEQ, heads_local, head_size), jnp.float32)

        def backward_block(running, block):
            keys_acc, values_acc = running
            query_blk, grad_blk, logsum_blk = block
            scores = jnp.einsum(
                "qhd,khd->hqk", query_blk, keys_seq, preferred_element_type=jnp.float32
            )
            scores = jnp.where(key_valid[None, None, :], scores, -1e30)
            attention = jnp.exp(scores - logsum_blk[..., None])
            attention_b = attention.astype(jnp.bfloat16)
            grad_attention = jnp.einsum(
                "qhd,khd->hqk", grad_blk, values_seq, preferred_element_type=jnp.float32
            )
            row_dots = jnp.sum(attention * grad_attention, axis=-1, keepdims=True)
            grad_scores = (attention * (grad_attention - row_dots)).astype(jnp.bfloat16)
            grad_query_blk = (
                softmax_scale
                * jnp.einsum(
                    "hqk,khd->qhd", grad_scores, keys_seq, preferred_element_type=jnp.float32
                )
            ).astype(jnp.bfloat16)
            keys_acc = keys_acc + jnp.einsum(
                "hqk,qhd->khd", grad_scores, query_blk, preferred_element_type=jnp.float32
            )
            values_acc = values_acc + jnp.einsum(
                "hqk,qhd->khd", attention_b, grad_blk, preferred_element_type=jnp.float32
            )
            return ((keys_acc, values_acc), grad_query_blk)

        (keys_acc, values_acc), grad_query_seq = lax.scan(
            backward_block, (initial, initial), (query_seq, grad_seq, logsum_seq)
        )
        return (grad_query_seq, keys_acc.astype(jnp.bfloat16), values_acc.astype(jnp.bfloat16))

    grad_query_all, grad_keys_all, grad_values_all = lax.map(
        backward_seq, (query5, keys4, values4, valid2, grad_heads5, logsum_all)
    )
    grad_query = grad_query_all.reshape(group_rows, local_width)
    grad_keys = grad_keys_all.reshape(group_rows, local_width)
    grad_values = grad_values_all.reshape(group_rows, local_width)
    grad_w_query = trans_times(grad_query, x_group)
    grad_w_key = trans_times(grad_keys, x_group)
    grad_w_value = trans_times(grad_values, x_group)
    grad_b_query_local = jnp.sum(grad_query.astype(jnp.float32), axis=0)
    grad_b_value_local = jnp.sum(grad_values.astype(jnp.float32), axis=0)
    part_query = times_plain(grad_query, attn_back[0])
    part_keys = times_plain(grad_keys, attn_back[1])
    part_values = times_plain(grad_values, attn_back[2])
    grad_inputs = grad_first + lax.psum_scatter(
        (part_query + part_keys + part_values).astype(jnp.bfloat16),
        "tensor",
        scatter_dimension=0,
        tiled=True,
    ).astype(jnp.float32)
    shard_wq, shard_wk, shard_wv, shard_wo, shard_wu, shard_wd = (
        lax.psum_scatter(grad_w_query, "dp", scatter_dimension=0, tiled=True),
        lax.psum_scatter(grad_w_key, "dp", scatter_dimension=0, tiled=True),
        lax.psum_scatter(grad_w_value, "dp", scatter_dimension=0, tiled=True),
        lax.psum_scatter(grad_w_out, "dp", scatter_dimension=0, tiled=True),
        lax.psum_scatter(grad_w_up, "dp", scatter_dimension=0, tiled=True),
        lax.psum_scatter(grad_w_down, "dp", scatter_dimension=0, tiled=True),
    )
    small_sums = lax.psum(
        (
            spread_into(grad_b_query_local, D, head_start),
            spread_into(grad_b_value_local, D, head_start),
            grad_b_out,
            spread_into(grad_b_up_local, FF, unit_start),
            grad_b_down,
            grad_gain_one,
            grad_shift_one,
            grad_gain_two,
            grad_shift_two,
            spread_into(grad_z_head_local, HEADS, tensor_pos * heads_local),
            grad_z_mha,
            hidden_part,
            spread_into(grad_z_int_local, FF, unit_start),
            grad_z_ffn,
        ),
        ("dp", "tensor"),
    )
    return (
        output,
        loss_value.reshape(1),
        grad_inputs,
        shard_wq,
        shard_wk,
        shard_wv,
        shard_wo,
        shard_wu,
        shard_wd,
        small_sums[0],
        small_sums[1],
        small_sums[2],
        small_sums[3],
        small_sums[4],
        small_sums[5],
        small_sums[6],
        small_sums[7],
        small_sums[8],
        small_sums[9],
        small_sums[10],
        small_sums[11],
        small_sums[12],
        small_sums[13],
    )


def solution(mesh):
    return jax.shard_map(
        on_device,
        mesh=mesh,
        in_specs=(
            P(("dp", "tensor"), None),
            P(("dp", "tensor"), None),
            P("dp"),
            P(("tensor", "dp"), None),
            P(("tensor", "dp"), None),
            P(("tensor", "dp"), None),
            P(("tensor", "dp"), None),
            P(("tensor", "dp"), None),
            P(("tensor", "dp"), None),
            P(),
            P(),
            P(),
            P(),
            P(),
            P(),
            P(),
            P(),
            P(),
            P(),
            P(),
            P(),
            P(),
            P(),
        ),
        out_specs=(
            P(("dp", "tensor"), None),
            P(),
            P(("dp", "tensor"), None),
            P(("tensor", "dp"), None),
            P(("tensor", "dp"), None),
            P(("tensor", "dp"), None),
            P(("tensor", "dp"), None),
            P(("tensor", "dp"), None),
            P(("tensor", "dp"), None),
            P(),
            P(),
            P(),
            P(),
            P(),
            P(),
            P(),
            P(),
            P(),
            P(),
            P(),
            P(),
            P(),
            P(),
        ),
        check_vma=False,
    )
```

profile of v0, /device:TPU:0, one launch (start us, length us, event | category | flops | bytes accessed | tf_op | source)
XLA Modules:
  0.0 964.6 jit_solution(14815683385056874799)
XLA Ops:
  11.3 25.0 %all_gather.37 = bf16[384,768]{1,0:T(8,128)(2,1)S(1)} all-gather(bf16[24,768]{1,0:T(8,128)(2,1)} %param.30), channel_id=1, replica_groups=mesh['dp'=16,'tensor'=2] {'dp'}, dimensions={0}, use_global_device_ids=true | all-gather | bytes 626688 | tf_op jit(solution)/shard_map/all_gather | solution.py:43
  36.3 19.3 %all_gather.38 = bf16[384,768]{1,0:T(8,128)(2,1)S(1)} all-gather(bf16[24,768]{1,0:T(8,128)(2,1)} %param.31), channel_id=1, replica_groups=mesh['dp'=16,'tensor'=2] {'dp'}, dimensions={0}, use_global_device_ids=true | all-gather | bytes 626688 | tf_op jit(solution)/shard_map/all_gather | solution.py:44
  55.6 20.4 %all_gather.39 = bf16[384,768]{1,0:T(8,128)(2,1)S(1)} all-gather(bf16[24,768]{1,0:T(8,128)(2,1)S(1)} %copy-done.31), channel_id=1, replica_groups=mesh['dp'=16,'tensor'=2] {'dp'}, dimensions={0}, use_global_device_ids=true | all-gather | bytes 626688 | tf_op jit(solution)/shard_map/all_gather | solution.py:45
  76.0 20.4 %all_gather.40 = bf16[384,768]{1,0:T(8,128)(2,1)} all-gather(bf16[24,768]{1,0:T(8,128)(2,1)S(1)} %copy-done.32), channel_id=1, replica_groups=mesh['dp'=16,'tensor'=2] {'dp'}, dimensions={0}, use_global_device_ids=true | all-gather | bytes 626688 | tf_op jit(solution)/shard_map/all_gather | solution.py:46
  96.4 2.4 multiply_convert_fusion.6
  102.8 48.4 %while.48 = (s32[]{:T(128)}, f32[2,512,6,64]{1,0,3,2:T(2,128)}, f32[2,6,512]{2,1,0:T(8,128)S(1)}, bf16[2,512,6,64]{1,3,2,0:T(8,128)(2,1)S(1)}, bf16[1024,6,64]{0...) while((s32[]{:T(128)}, f32[2,512,6,64]{1,0,3,2:T(2,128)}, ...), condition=%wide.region_3.4_spmd.clone, body=%wide.region_0.3_spmd.clone.sunk | while | flops 833630208 | bytes 43761780 | solution.py:138
  103.5 1.9 select_reduce_fusion.2
  105.4 2.8 fusion.145
  108.2 3.0 fusion.146
  112.0 15.0 %dynamic_update_slice.55 = f32[2,512,6,64]{1,0,3,2:T(2,128)} dynamic-update-slice(f32[2,512,6,64]{1,0,3,2:T(2,128)} %get-tuple-element.493, f32[1,512,6,64]{1,0,3,2:T(1,128)S(1)} %copy.97, s32[]{:T(128)S(6)} %copy.104, s32[]{:T(128)} %constant.77.clone.1..sunk, s32[]{:T(128)} %constant.77.clone.1..sunk, s32[]{:T(128)} %constant.77.clone.1..sunk) | dynamic-update-slice | bytes 1572868 | tf_op jit(solution)/shard_map/while/body/eval_jaxpr/while/body/jit(dynamic_update_index_in_dim)/dynamic_update_slice | solution.py:138
  127.6 1.9 select_reduce_fusion.2
  129.6 2.8 fusion.145
  132.4 3.0 fusion.146
  136.2 15.0 %dynamic_update_slice.55 = f32[2,512,6,64]{1,0,3,2:T(2,128)} dynamic-update-slice(f32[2,512,6,64]{1,0,3,2:T(2,128)} %get-tuple-element.493, f32[1,512,6,64]{1,0,3,2:T(1,128)S(1)} %copy.97, s32[]{:T(128)S(6)} %copy.104, s32[]{:T(128)} %constant.77.clone.1..sunk, s32[]{:T(128)} %constant.77.clone.1..sunk, s32[]{:T(128)} %constant.77.clone.1..sunk) | dynamic-update-slice | bytes 1572868 | tf_op jit(solution)/shard_map/while/body/eval_jaxpr/while/body/jit(dynamic_update_index_in_dim)/dynamic_update_slice | solution.py:138
  152.1 1.8 copy.94
  153.9 2.7 fusion.69
  159.0 39.8 %reduce-scatter.11.cloned.1.call-done = f32[512,768]{1,0:T(8,128)} async-done(((f32[1024,768]{1,0:T(8,128)}), f32[512,768]{1,0:T(8,128)}) %reduce-scatter.11.cloned.1.call-update) | async-done | bytes 1572880 | tf_op jit(solution)/shard_map/reduce_scatter | solution.py:148
  198.8 1.9 fusion.74
  203.5 26.3 %all-gather.9.cloned.1.call-done = bf16[1024,768]{1,0:T(8,128)(2,1)} async-done(((bf16[512,768]{1,0:T(8,128)(2,1)}), bf16[1024,768]{1,0:T(8,128)(2,1)}) %all-gather.9.cloned.1.call-update) | async-done | bytes 1572880 | tf_op jit(solution)/shard_map/all_gather | solution.py:154
  229.8 20.1 %multiply_convert_fusion.1 = (bf16[1024,1536]{1,0:T(8,128)(2,1)}, f32[1024,1536]{1,0:T(8,128)}, f32[1024,1536]{1,0:T(8,128)}) fusion(f32[1536]{0:T(1024)S(1)} %dynamic_slice.60, f32[1536]{0:T(1024)S(1)} %dynamic_slice.59, bf16[1024,768]{1,0:T(8,128)(2,1)} %all-gather.9.cloned.1.call-done, bf16[1536,768]{1,0:T(8,128)(2,1)} %all-gather.11.cloned.1.call-done), kind=kOutput, calls=%fused_computation.73 | convolution fusion | flops 2521300992 | bytes 19673088 | tf_op jit(solution)/shard_map/dot_general | solution.py:30
  249.9 25.1 %all-gather.13.cloned.1.call-done = bf16[1536,768]{1,0:T(8,128)(2,1)} async-done(((bf16[96,768]{1,0:T(8,128)(2,1)}), bf16[1536,768]{1,0:T(8,128)(2,1)}) %all-gather.13.cloned.1.call-update) | async-done | bytes 2359312 | tf_op jit(solution)/shard_map/all_gather | solution.py:53
  275.0 6.9 fusion.75
  283.3 38.9 %psum.113 = f32[]{:T(128)} all-reduce(f32[]{:T(128)} %get-tuple-element.352), channel_id=1, replica_groups=mesh['dp'=16,'tensor'=2] {'dp','tensor'}, use_global_device_ids=true, to_apply=%region_13.14 | all-reduce | flops 1 | bytes 8 | tf_op jit(solution)/shard_map/psum | solution.py:168
  322.9 2.4 reduce-scatter.13.cloned.1.call-done
  325.2 2.0 fusion.72
  328.4 2.8 multiply_reduce_fusion.7
  334.8 26.9 %all-gather.15.cloned.1.call-done = bf16[1024,768]{1,0:T(8,128)(2,1)} async-done(((bf16[512,768]{1,0:T(8,128)(2,1)}), bf16[1024,768]{1,0:T(8,128)(2,1)}) %all-gather.15.cloned.1.call-update) | async-done | bytes 1572880 | tf_op jit(solution)/shard_map/all_gather | solution.py:182
  361.7 10.6 %convert_reduce_fusion = (f32[1536]{0:T(1024)}, bf16[1024,1536]{1,0:T(8,128)(2,1)S(1)}, f32[1536]{0:T(1024)}) fusion(f32[1024,1536]{1,0:T(8,128)} %get-tuple-element.357, f32[1536]{0:T(1024)S(1)} %dynamic_slice.60, f32[1024,1536]{1,0:T(8,128)} %get-tuple-element.368, f32[1536]{0:T(1024)S(1)} %dynamic_slice.59, ...), kind=kOutput, calls=%fused_computation.71 | convolution fusion | flops 2448946176 | bytes 19685376 | tf_op jit(solution)/shard_map/dot_general | solution.py:30
  373.9 4.2 fusion.76
  378.2 43.3 %reduce-scatter.15.cloned.1.call-done = f32[512,768]{1,0:T(8,128)} async-done(((f32[1024,768]{1,0:T(8,128)}), f32[512,768]{1,0:T(8,128)}) %reduce-scatter.15.cloned.1.call-update) | async-done | bytes 1572880 | tf_op jit(solution)/shard_map/reduce_scatter | solution.py:190
  421.5 3.3 multiply_reduce_fusion.8
  426.6 1.8 convert_reduce_fusion.2
  430.3 25.5 %all-gather.17.cloned.1.call-done = bf16[1024,768]{1,0:T(8,128)(2,1)} async-done(((bf16[512,768]{1,0:T(8,128)(2,1)}), bf16[1024,768]{1,0:T(8,128)(2,1)}) %all-gather.17.cloned.1.call-update) | async-done | bytes 1572880 | tf_op jit(solution)/shard_map/all_gather | solution.py:199
  455.8 4.8 multiply_reduce_fusion.6
  460.6 1.9 copy.61
  462.4 2.5 reshape.209
  464.9 2.1 multiply_convert_fusion.2
  467.1 48.7 %while.49 = (s32[]{:T(128)}, f32[1024,6,64]{0,2,1:T(8,128)S(1)}, f32[1024,6,64]{0,2,1:T(8,128)}, bf16[2,512,6,64]{1,3,2,0:T(8,128)(2,1)}, bf16[2,512,6,64]{1,3,2...) while((s32[]{:T(128)}, f32[1024,6,64]{0,2,1:T(8,128)S(1)}, ...), condition=%wide.region_21.22_spmd.clone, body=%wide.region_19.21_spmd.clone.sunk | while | flops 2052993024 | bytes 142831920 | solution.py:238
  467.9 2.8 fusion.156
  470.7 3.5 bitcast_add_fusion.5
  474.2 4.6 multiply_reduce_fusion.16
  478.9 4.6 multiply_convert_fusion.12
  483.5 5.9 fusion.158
  491.5 2.8 fusion.156
  494.4 4.6 bitcast_add_fusion.5
  499.0 4.6 multiply_reduce_fusion.16
  503.6 4.6 multiply_convert_fusion.12
  508.2 5.9 fusion.158
  518.2 1.9 convert_reduce_fusion.3
  522.5 2.3 add_convert_fusion.1
  526.1 6.7 fusion.83
  534.2 6.7 fusion.82
  542.9 1.9 fusion.68
  544.8 3.6 fusion.81
  548.5 1.9 fusion.80
  550.7 3.3 fusion.79
  558.0 5.1 multiply_reduce_fusion.3
  563.2 42.5 %all-reduce = (f32[]{:T(128)}, f32[768]{0:T(1024)}, f32[768]{0:T(1024)}, f32[768]{0:T(1024)}, f32[3072]{0:T(1024)}, /*index=5*/f32[768]{0:T(1024)}, f32[768]{0:T...) all-reduce(f32[]{:T(128)} %get-tuple-element.284, ...), channel_id=1, replica_groups=mesh['dp'=16,'tensor'=2] {'dp','tensor'}, use_global_device_ids=true, to_apply=%region_11.12 | all-reduce | flops 13071 | bytes 104568 | tf_op jit(solution)/shard_map/psum | solution.py:168
  606.3 24.8 %reduce-scatter.29.cloned.1.call-done = f32[96,768]{1,0:T(8,128)} async-done(((f32[1536,768]{1,0:T(8,128)}), f32[96,768]{1,0:T(8,128)}) %reduce-scatter.29.cloned.1.call-update) | async-done | bytes 294928 | tf_op jit(solution)/shard_map/reduce_scatter | solution.py:269
  631.1 79.6 %reduce-scatter.27.cloned.1.call-done = f32[96,768]{1,0:T(8,128)} async-done(((f32[1536,768]{1,0:T(8,128)}), f32[96,768]{1,0:T(8,128)}) %reduce-scatter.27.cloned.1.call-update) | async-done | bytes 294928 | tf_op jit(solution)/shard_map/reduce_scatter | solution.py:268
  710.7 61.3 %reduce-scatter.25.cloned.1.call-done = f32[24,768]{1,0:T(8,128)} async-done(((f32[384,768]{1,0:T(8,128)}), f32[24,768]{1,0:T(8,128)}) %reduce-scatter.25.cloned.1.call-update) | async-done | bytes 73744 | tf_op jit(solution)/shard_map/reduce_scatter | solution.py:267
  772.0 61.2 %reduce-scatter.23.cloned.1.call-done = f32[24,768]{1,0:T(8,128)} async-done(((f32[384,768]{1,0:T(8,128)}), f32[24,768]{1,0:T(8,128)}) %reduce-scatter.23.cloned.1.call-update) | async-done | bytes 73744 | tf_op jit(solution)/shard_map/reduce_scatter | solution.py:266
  833.3 61.2 %reduce-scatter.21.cloned.1.call-done = f32[24,768]{1,0:T(8,128)} async-done(((f32[384,768]{1,0:T(8,128)}), f32[24,768]{1,0:T(8,128)}) %reduce-scatter.21.cloned.1.call-update) | async-done | bytes 73744 | tf_op jit(solution)/shard_map/reduce_scatter | solution.py:265
  894.4 61.3 %reduce-scatter.19.cloned.1.call-done = f32[24,768]{1,0:T(8,128)} async-done(((f32[384,768]{1,0:T(8,128)}), f32[24,768]{1,0:T(8,128)}) %reduce-scatter.19.cloned.1.call-update) | async-done | bytes 73744 | tf_op jit(solution)/shard_map/reduce_scatter | solution.py:264
  (248 shorter events, 42.5 us)
Async XLA Ops:
  8.0 47.6 %copy-start.31 = (bf16[24,768]{1,0:T(8,128)(2,1)S(1)}, bf16[24,768]{1,0:T(8,128)(2,1)}, u32[]{:S(2)}) copy-start(bf16[24,768]{1,0:T(8,128)(2,1)} %param.32) | copy-start | bytes 110596
  8.0 68.0 %copy-start.32 = (bf16[24,768]{1,0:T(8,128)(2,1)S(1)}, bf16[24,768]{1,0:T(8,128)(2,1)}, u32[]{:S(2)}) copy-start(bf16[24,768]{1,0:T(8,128)(2,1)} %param.33) | copy-start | bytes 110596
  8.0 88.4 %all-gather.7.cloned.1.call-start = ((), (), s32[]{:S(2)}) async-start(), calls=%async_computation.10 | async-start | bytes 2359296 | tf_op jit(solution)/shard_map/all_gather | solution.py:112
  8.8 190.0 %reduce-scatter.11.cloned.1.call-start = ((), (), s32[]{:S(2)}) async-start(), calls=%async_computation.11 | async-start | bytes 4718592 | tf_op jit(solution)/shard_map/reduce_scatter | solution.py:148
  11.1 87.8 %copy-start.59 = (f32[6]{0:T(128)}, f32[6]{0:T(128)S(1)}, u32[]{:S(2)}) copy-start(f32[6]{0:T(128)S(1)} %dynamic_slice.58) | copy-start | bytes 76
  11.3 142.7 %copy-start.35 = (f32[384]{0:T(512)}, f32[384]{0:T(512)S(1)}, u32[]{:S(2)}) copy-start(f32[384]{0:T(512)S(1)} %mul.331) | copy-start | bytes 4612
  36.3 60.1 %copy-start.23 = (bf16[384,768]{1,0:T(8,128)(2,1)}, bf16[384,768]{1,0:T(8,128)(2,1)S(1)}, u32[]{:S(2)}) copy-start(bf16[384,768]{1,0:T(8,128)(2,1)S(1)} %all_gather.37) | copy-start | bytes 1769476
  55.6 44.3 %copy-start.27 = (bf16[384,768]{1,0:T(8,128)(2,1)}, bf16[384,768]{1,0:T(8,128)(2,1)S(1)}, u32[]{:S(2)}) copy-start(bf16[384,768]{1,0:T(8,128)(2,1)S(1)} %all_gather.38) | copy-start | bytes 1769476
  76.0 26.0 %copy-start.25 = (bf16[384,768]{1,0:T(8,128)(2,1)}, bf16[384,768]{1,0:T(8,128)(2,1)S(1)}, u32[]{:S(2)}) copy-start(bf16[384,768]{1,0:T(8,128)(2,1)S(1)} %all_gather.39) | copy-start | bytes 1769476
  151.2 5.5 copy-start.1
  151.2 5.5 copy-start.4
  153.9 274.7 %copy-start.8 = (f32[48,8,2,512]{3,1,2,0:T(8,128)}, f32[48,8,2,512]{3,1,2,0:T(8,128)S(1)}, u32[]{:S(2)}) copy-start(f32[48,8,2,512]{3,1,2,0:T(8,128)S(1)} %copy.94) | copy-start | bytes 4718596
  156.7 2.3 copy-start.48
  156.7 42.1 %copy-start.40 = (f32[768]{0:T(1024)S(1)}, f32[768]{0:T(1024)}, u32[]{:S(2)}) copy-start(f32[768]{0:T(1024)} %param.38) | copy-start | bytes 9220
  156.7 46.7 %all-gather.11.cloned.1.call-start = ((), (), s32[]{:S(2)}) async-start(), calls=%async_computation.13 | async-start | bytes 2506752 | tf_op jit(solution)/shard_map/all_gather | solution.py:52
  157.3 72.5 %all-gather.9.cloned.1.call-start = ((), (), s32[]{:S(2)}) async-start(), calls=%async_computation.12 | async-start | bytes 2359296 | tf_op jit(solution)/shard_map/all_gather | solution.py:154
  201.4 1.9 copy-start.57
  202.7 72.3 %all-gather.13.cloned.1.call-start = ((), (), s32[]{:S(2)}) async-start(), calls=%async_computation.14 | async-start | bytes 2506752 | tf_op jit(solution)/shard_map/all_gather | solution.py:53
  203.2 122.0 %reduce-scatter.13.cloned.1.call-start = ((), (), s32[]{:S(2)}) async-start(), calls=%async_computation.15 | async-start | bytes 4718592 | tf_op jit(solution)/shard_map/reduce_scatter | solution.py:160
  281.8 43.4 %copy-start.42 = (f32[768]{0:T(1024)S(1)}, f32[768]{0:T(1024)}, u32[]{:S(2)}) copy-start(f32[768]{0:T(1024)} %param.40) | copy-start | bytes 9220
  281.9 79.8 %all-gather.15.cloned.1.call-start = ((), (), s32[]{:S(2)}) async-start(), calls=%async_computation.16 | async-start | bytes 2359296 | tf_op jit(solution)/shard_map/all_gather | solution.py:182
  331.8 89.6 %copy-start.33 = (f32[512]{0:T(512)}, f32[512]{0:T(512)S(1)}, u32[]{:S(2)}) copy-start(f32[512]{0:T(512)S(1)} %negate_multiply_fusion.2) | copy-start | bytes 6148
  334.7 86.8 %reduce-scatter.15.cloned.1.call-start = ((), (), s32[]{:S(2)}) async-start(), calls=%async_computation.17 | async-start | bytes 4718592 | tf_op jit(solution)/shard_map/reduce_scatter | solution.py:190
  361.7 12.2 %copy-start.61 = (bf16[1536,768]{1,0:T(8,128)(2,1)S(1)}, bf16[1536,768]{1,0:T(8,128)(2,1)}, u32[]{:S(2)}) copy-start(bf16[1536,768]{1,0:T(8,128)(2,1)} %all-gather.11.cloned.1.call-done) | copy-start | bytes 7077892
  378.1 77.6 %all-gather.17.cloned.1.call-start = ((), (), s32[]{:S(2)}) async-start(), calls=%async_computation.18 | async-start | bytes 2359296 | tf_op jit(solution)/shard_map/all_gather | solution.py:199
  425.4 3.0 copy-start.37
  428.4 129.5 %reduce-scatter.17.cloned.1.call-start = ((), (), s32[]{:S(2)}) async-start(), calls=%async_computation.19 | async-start | bytes 2359296 | tf_op jit(solution)/shard_map/reduce_scatter | solution.py:257
  462.4 2.5 copy-start.60
  464.9 2.2 copy-start.2
  467.2 3.5 copy-start.6
  483.5 5.9 copy-start
  483.5 5.9 copy-start.5
  490.8 3.5 copy-start.6
  508.2 5.9 copy-start
  508.2 5.9 copy-start.5
  515.9 4.1 copy-start.21
  518.1 3.0 copy-start.19
  518.1 1.9 copy-start.28
  520.0 2.4 copy-start.17
  524.7 106.4 %reduce-scatter.29.cloned.1.call-start = ((), (), s32[]{:S(2)}) async-start(), calls=%async_computation.25 | async-start | bytes 5013504 | tf_op jit(solution)/shard_map/reduce_scatter | solution.py:269
  532.9 177.8 %reduce-scatter.27.cloned.1.call-start = ((), (), s32[]{:S(2)}) async-start(), calls=%async_computation.24 | async-start | bytes 5013504 | tf_op jit(solution)/shard_map/reduce_scatter | solution.py:268
  541.0 231.0 %reduce-scatter.25.cloned.1.call-start = ((), (), s32[]{:S(2)}) async-start(), calls=%async_computation.23 | async-start | bytes 1253376 | tf_op jit(solution)/shard_map/reduce_scatter | solution.py:267
  544.8 3.7 copy-start.22
  544.8 3.7 copy-start.63
  544.8 288.5 %reduce-scatter.23.cloned.1.call-start = ((), (), s32[]{:S(2)}) async-start(), calls=%async_computation.22 | async-start | bytes 1253376 | tf_op jit(solution)/shard_map/reduce_scatter | solution.py:266
  548.4 2.3 copy-start.20
  548.4 346.0 %reduce-scatter.21.cloned.1.call-start = ((), (), s32[]{:S(2)}) async-start(), calls=%async_computation.21 | async-start | bytes 1253376 | tf_op jit(solution)/shard_map/reduce_scatter | solution.py:265
  550.4 4.5 copy-start.55
  550.4 4.8 copy-start.54
  550.4 5.2 copy-start.53
  550.4 405.3 %reduce-scatter.19.cloned.1.call-start = ((), (), s32[]{:S(2)}) async-start(), calls=%async_computation.20 | async-start | bytes 1253376 | tf_op jit(solution)/shard_map/reduce_scatter | solution.py:264
  550.7 7.2 copy-start.14
  554.1 3.8 copy-start.11
  554.1 3.8 copy-start.34
  554.1 3.8 copy-start.38
  554.1 3.8 copy-start.41
  554.1 3.8 copy-start.43
  554.1 3.8 copy-start.49
  558.0 5.2 copy-start.44
  558.0 5.2 copy-start.45
  558.0 5.1 copy-start.46
  558.0 5.1 copy-start.47
  558.0 5.1 copy-start.51
  558.0 5.1 copy-start.52
  (24 other events, 32.3 us)
Sparse Core Ops, SparseCore 0:
  10.4 29.9 all-gather.6
  156.8 41.9 reduce-scatter.10
  282.0 43.1 reduce-scatter.12
  428.5 27.2 all-gather.16
  524.9 26.0 reduce-scatter.16
  555.3 75.8 reduce-scatter.28
  636.0 74.6 reduce-scatter.26
  714.9 57.1 reduce-scatter.24
  776.2 56.9 reduce-scatter.22
  837.3 57.0 reduce-scatter.20
  898.6 57.0 reduce-scatter.18
Sparse Core Ops, SparseCore 1:
  159.7 41.1 all-gather.10
  202.9 26.8 all-gather.8
  232.2 42.7 all-gather.12
  334.8 26.8 all-gather.14
  378.2 43.2 reduce-scatter.14
where the time goes:
time: 976 us; the launch traced here: 965 us
  waiting for transfers between devices  541 us (55%)
  blocking collectives  167 us (17%)
  matrix products  129 us (13%)
  local copies, waits for them, and re-layouts  59.1 us (6%)
  other arithmetic  45.3 us (5%)
  between operations  22 us (2%)
    psum x2, blocking collectives, on_device(): lax.psum((jnp.sum(valid_own.astype(jnp.float32)), jnp.sum(masked * masked...  81.4 us
    reduce_scatter x1, waiting for transfers between devices, on_device(): lax.psum_scatter(grad_w_up, 'dp', scatter_dimension=0, tiled=True)  79.6 us
    reduce_scatter x1, waiting for transfers between devices, on_device(): lax.psum_scatter(grad_w_out, 'dp', scatter_dimension=0, tiled=True)  61.3 us
    reduce_scatter x1, waiting for transfers between devices, on_device(): lax.psum_scatter(grad_w_query, 'dp', scatter_dimension=0, tiled=True)  61.3 us
    reduce_scatter x1, waiting for transfers between devices, on_device(): lax.psum_scatter(grad_w_value, 'dp', scatter_dimension=0, tiled=True)  61.2 us
    reduce_scatter x1, waiting for transfers between devices, on_device(): lax.psum_scatter(grad_w_key, 'dp', scatter_dimension=0, tiled=True)  61.2 us
    reduce_scatter x1, waiting for transfers between devices, on_device(): lax.psum_scatter(times_plain(grad_upper, ffn_back[0]), 'tensor', scatter_...  43.3 us
    reduce_scatter x1, waiting for transfers between devices, on_device(): lax.psum_scatter(times_plain(gated, wo_full), 'tensor', scatter_dimension...  39.8 us
  transfers between devices with their start and end apart: 16, of which 13 were waited for; matrix products, arithmetic and copies ran while one was open for 6% of the time, Pallas kernels for 0%

commit v1 on v0

--- a/solution.py
+++ b/solution.py
@@ -166,7 +166,7 @@
     residue = output - teacher.astype(jnp.float32)
     masked = jnp.where(valid_own[:, None], residue, 0.0)
     valid_count, square_sum = lax.psum(
-        (jnp.sum(valid_own.astype(jnp.float32)), jnp.sum(masked * masked)), ("dp", "tensor")
+        lax.psum((jnp.sum(valid_own.astype(jnp.float32)), jnp.sum(masked * masked)), "tensor"), "dp"
     )
     loss_value = square_sum / (D * valid_count)
     tokens_all = group_rows * lax.axis_size("dp")

time: 976 us -> 982 us (level)
  blocking collectives: 167 us -> 201 us
  waiting for transfers between devices: 541 us -> 509 us
    psum x0 -> x3, blocking collectives: none -> 103 us  [the longest x2 63.7 us: on_device(): lax.psum(lax.psum((jnp.sum(valid_own.astype(jnp.float32)), jnp.sum(masked...]
    psum x2, blocking collectives: 81.4 us -> 11.1 us  [on_device(): lax.psum((jnp.sum(valid_own.astype(jnp.float32)), jnp.sum(masked * masked...]
    reduce_scatter x1, waiting for transfers between devices: 24.8 us -> 0.01 us  [on_device(): lax.psum_scatter(grad_w_down, 'dp', scatter_dimension=0, tiled=True)]
  transfers between devices with their start and end apart: 16 -> 16, of which waited for: 13 -> 12; matrix products, arithmetic and copies ran while one was open for 6% -> 6% of each run, Pallas kernels for 0% -> 0%
where the time goes in v1:
time: 982 us; the launch traced here: 970 us
  waiting for transfers between devices  509 us (52%)
  blocking collectives  201 us (20%)
  matrix products  129 us (13%)
  local copies, waits for them, and re-layouts  64.5 us (7%)
  other arithmetic  42 us (4%)
  between operations  21.8 us (2%)
    reduce_scatter x1, waiting for transfers between devices, on_device(): lax.psum_scatter(grad_w_up, 'dp', scatter_dimension=0, tiled=True)  73.5 us
    psum x2, blocking collectives, on_device(): lax.psum(lax.psum((jnp.sum(valid_own.astype(jnp.float32)), jnp.sum(masked...  63.7 us
    reduce_scatter x1, waiting for transfers between devices, on_device(): lax.psum_scatter(grad_w_query, 'dp', scatter_dimension=0, tiled=True)  61.4 us
    reduce_scatter x1, waiting for transfers between devices, on_device(): lax.psum_scatter(grad_w_out, 'dp', scatter_dimension=0, tiled=True)  61.4 us
    reduce_scatter x1, waiting for transfers between devices, on_device(): lax.psum_scatter(grad_w_value, 'dp', scatter_dimension=0, tiled=True)  61.2 us
    reduce_scatter x1, waiting for transfers between devices, on_device(): lax.psum_scatter(grad_w_key, 'dp', scatter_dimension=0, tiled=True)  61 us
    reduce_scatter x1, waiting for transfers between devices, on_device(): lax.psum_scatter(times_plain(grad_upper, ffn_back[0]), 'tensor', scatter_...  43.3 us
    reduce_scatter x1, waiting for transfers between devices, on_device(): lax.psum_scatter(times_plain(gated, wo_full), 'tensor', scatter_dimension...  39.9 us
  transfers between devices with their start and end apart: 16, of which 12 were waited for; matrix products, arithmetic and copies ran while one was open for 6% of the time, Pallas kernels for 0%

profile of v1, /device:TPU:0, one launch (start us, length us, event | category | flops | bytes accessed | tf_op | source)
XLA Modules:
  0.0 969.6 jit_solution(3657630726280060253)
XLA Ops:
  11.3 25.0 %all_gather.37 = bf16[384,768]{1,0:T(8,128)(2,1)S(1)} all-gather(bf16[24,768]{1,0:T(8,128)(2,1)} %param.30), channel_id=1, replica_groups=mesh['dp'=16,'tensor'=2] {'dp'}, dimensions={0}, use_global_device_ids=true | all-gather | bytes 626688 | tf_op jit(solution)/shard_map/all_gather | solution.py:43
  36.3 19.3 %all_gather.38 = bf16[384,768]{1,0:T(8,128)(2,1)S(1)} all-gather(bf16[24,768]{1,0:T(8,128)(2,1)} %param.31), channel_id=1, replica_groups=mesh['dp'=16,'tensor'=2] {'dp'}, dimensions={0}, use_global_device_ids=true | all-gather | bytes 626688 | tf_op jit(solution)/shard_map/all_gather | solution.py:44
  55.6 21.8 %all_gather.39 = bf16[384,768]{1,0:T(8,128)(2,1)} all-gather(bf16[24,768]{1,0:T(8,128)(2,1)S(1)} %copy-done.33), channel_id=1, replica_groups=mesh['dp'=16,'tensor'=2] {'dp'}, dimensions={0}, use_global_device_ids=true | all-gather | bytes 626688 | tf_op jit(solution)/shard_map/all_gather | solution.py:45
  77.4 20.4 %all_gather.40 = bf16[384,768]{1,0:T(8,128)(2,1)} all-gather(bf16[24,768]{1,0:T(8,128)(2,1)S(1)} %copy-done.34), channel_id=1, replica_groups=mesh['dp'=16,'tensor'=2] {'dp'}, dimensions={0}, use_global_device_ids=true | all-gather | bytes 626688 | tf_op jit(solution)/shard_map/all_gather | solution.py:46
  97.8 2.4 multiply_convert_fusion.6
  104.4 48.4 %while.48 = (s32[]{:T(128)}, f32[2,512,6,64]{1,0,3,2:T(2,128)}, f32[2,6,512]{2,1,0:T(8,128)S(1)}, bf16[2,512,6,64]{1,3,2,0:T(8,128)(2,1)S(1)}, bf16[1024,6,64]{0...) while((s32[]{:T(128)}, f32[2,512,6,64]{1,0,3,2:T(2,128)}, ...), condition=%wide.region_3.4_spmd.clone, body=%wide.region_0.3_spmd.clone.sunk | while | flops 833630208 | bytes 43761780 | solution.py:138
  105.0 1.9 select_reduce_fusion.2
  107.0 2.8 fusion.145
  109.8 3.0 fusion.146
  113.6 15.0 %dynamic_update_slice.55 = f32[2,512,6,64]{1,0,3,2:T(2,128)} dynamic-update-slice(f32[2,512,6,64]{1,0,3,2:T(2,128)} %get-tuple-element.493, f32[1,512,6,64]{1,0,3,2:T(1,128)S(1)} %copy.97, s32[]{:T(128)S(6)} %copy.104, s32[]{:T(128)} %constant.77.clone.1..sunk, s32[]{:T(128)} %constant.77.clone.1..sunk, s32[]{:T(128)} %constant.77.clone.1..sunk) | dynamic-update-slice | bytes 1572868 | tf_op jit(solution)/shard_map/while/body/eval_jaxpr/while/body/jit(dynamic_update_index_in_dim)/dynamic_update_slice | solution.py:138
  129.2 1.9 select_reduce_fusion.2
  131.2 2.8 fusion.145
  134.0 3.0 fusion.146
  137.8 15.0 %dynamic_update_slice.55 = f32[2,512,6,64]{1,0,3,2:T(2,128)} dynamic-update-slice(f32[2,512,6,64]{1,0,3,2:T(2,128)} %get-tuple-element.493, f32[1,512,6,64]{1,0,3,2:T(1,128)S(1)} %copy.97, s32[]{:T(128)S(6)} %copy.104, s32[]{:T(128)} %constant.77.clone.1..sunk, s32[]{:T(128)} %constant.77.clone.1..sunk, s32[]{:T(128)} %constant.77.clone.1..sunk) | dynamic-update-slice | bytes 1572868 | tf_op jit(solution)/shard_map/while/body/eval_jaxpr/while/body/jit(dynamic_update_index_in_dim)/dynamic_update_slice | solution.py:138
  152.8 2.6 copy.94
  156.6 2.8 fusion.69
  161.6 39.9 %reduce-scatter.11.cloned.1.call-done = f32[512,768]{1,0:T(8,128)} async-done(((f32[1024,768]{1,0:T(8,128)}), f32[512,768]{1,0:T(8,128)}) %reduce-scatter.11.cloned.1.call-update) | async-done | bytes 1572880 | tf_op jit(solution)/shard_map/reduce_scatter | solution.py:148
  206.0 26.4 %all-gather.9.cloned.1.call-done = bf16[1024,768]{1,0:T(8,128)(2,1)} async-done(((bf16[512,768]{1,0:T(8,128)(2,1)}), bf16[1024,768]{1,0:T(8,128)(2,1)}) %all-gather.9.cloned.1.call-update) | async-done | bytes 1572880 | tf_op jit(solution)/shard_map/all_gather | solution.py:154
  232.4 20.3 %multiply_convert_fusion.1 = (bf16[1024,1536]{1,0:T(8,128)(2,1)}, f32[1024,1536]{1,0:T(8,128)}, f32[1024,1536]{1,0:T(8,128)}) fusion(f32[1536]{0:T(1024)S(1)} %dynamic_slice.60, f32[1536]{0:T(1024)S(1)} %dynamic_slice.59, bf16[1024,768]{1,0:T(8,128)(2,1)} %all-gather.9.cloned.1.call-done, bf16[1536,768]{1,0:T(8,128)(2,1)} %all-gather.11.cloned.1.call-done), kind=kOutput, calls=%fused_computation.73 | convolution fusion | flops 2521300992 | bytes 19673088 | tf_op jit(solution)/shard_map/dot_general | solution.py:30
  252.6 24.9 %all-gather.13.cloned.1.call-done = bf16[1536,768]{1,0:T(8,128)(2,1)} async-done(((bf16[96,768]{1,0:T(8,128)(2,1)}), bf16[1536,768]{1,0:T(8,128)(2,1)}) %all-gather.13.cloned.1.call-update) | async-done | bytes 2359312 | tf_op jit(solution)/shard_map/all_gather | solution.py:53
  277.5 6.9 fusion.75
  285.8 5.5 psum.128
  291.4 30.6 %psum.129 = f32[]{:T(128)} all-reduce(f32[]{:T(128)} %psum.128), channel_id=1, replica_groups=mesh['dp'=16,'tensor'=2] {'dp'}, use_global_device_ids=true, to_apply=%region_15.16 | all-reduce | flops 1 | bytes 8 | tf_op jit(solution)/shard_map/psum | solution.py:168
  322.7 3.8 reduce-scatter.13.cloned.1.call-done
  326.5 2.0 fusion.72
  329.6 2.7 multiply_reduce_fusion.7
  335.2 26.7 %all-gather.15.cloned.1.call-done = bf16[1024,768]{1,0:T(8,128)(2,1)} async-done(((bf16[512,768]{1,0:T(8,128)(2,1)}), bf16[1024,768]{1,0:T(8,128)(2,1)}) %all-gather.15.cloned.1.call-update) | async-done | bytes 1572880 | tf_op jit(solution)/shard_map/all_gather | solution.py:182
  361.9 10.5 %convert_reduce_fusion = (f32[1536]{0:T(1024)}, bf16[1024,1536]{1,0:T(8,128)(2,1)S(1)}, f32[1536]{0:T(1024)}) fusion(f32[1024,1536]{1,0:T(8,128)} %get-tuple-element.356, f32[1536]{0:T(1024)S(1)} %dynamic_slice.60, f32[1024,1536]{1,0:T(8,128)} %get-tuple-element.368, f32[1536]{0:T(1024)S(1)} %dynamic_slice.59, ...), kind=kOutput, calls=%fused_computation.71 | convolution fusion | flops 2448946176 | bytes 19685376 | tf_op jit(solution)/shard_map/dot_general | solution.py:30
  374.1 4.3 fusion.76
  378.4 43.3 %reduce-scatter.15.cloned.1.call-done = f32[512,768]{1,0:T(8,128)} async-done(((f32[1024,768]{1,0:T(8,128)}), f32[512,768]{1,0:T(8,128)}) %reduce-scatter.15.cloned.1.call-update) | async-done | bytes 1572880 | tf_op jit(solution)/shard_map/reduce_scatter | solution.py:190
  421.7 2.8 multiply_reduce_fusion.8
  427.0 2.9 multiply_reduce_fusion.3
  430.2 3.1 copy.65
  433.3 24.0 %all-gather.17.cloned.1.call-done = bf16[1024,768]{1,0:T(8,128)(2,1)} async-done(((bf16[512,768]{1,0:T(8,128)(2,1)}), bf16[1024,768]{1,0:T(8,128)(2,1)}) %all-gather.17.cloned.1.call-update) | async-done | bytes 1572880 | tf_op jit(solution)/shard_map/all_gather | solution.py:199
  457.3 4.6 multiply_reduce_fusion.6
  462.0 3.1 copy.61
  465.0 3.4 reshape.209
  468.5 2.1 multiply_convert_fusion.2
  471.6 48.7 %while.49 = (s32[]{:T(128)}, f32[1024,6,64]{0,2,1:T(8,128)S(1)}, f32[1024,6,64]{0,2,1:T(8,128)}, bf16[2,512,6,64]{1,3,2,0:T(8,128)(2,1)}, bf16[2,512,6,64]{1,3,2...) while((s32[]{:T(128)}, f32[1024,6,64]{0,2,1:T(8,128)S(1)}, ...), condition=%wide.region_23.24_spmd.clone, body=%wide.region_21.23_spmd.clone.sunk | while | flops 2052993024 | bytes 139686160 | solution.py:238
  472.3 2.9 fusion.156
  475.2 3.5 bitcast_add_fusion.5
  478.7 4.6 multiply_reduce_fusion.16
  483.4 4.6 multiply_convert_fusion.12
  488.0 5.9 fusion.158
  496.0 2.9 fusion.156
  498.9 4.6 bitcast_add_fusion.5
  503.5 4.6 multiply_reduce_fusion.16
  508.2 4.6 multiply_convert_fusion.12
  512.8 5.9 fusion.158
  526.9 2.3 add_convert_fusion.1
  530.6 6.7 fusion.83
  538.7 6.7 fusion.82
  547.3 1.9 fusion.68
  549.3 3.6 fusion.81
  555.2 3.3 fusion.79
  558.6 5.6 psum.126
  564.8 33.1 %psum.127 = f32[]{:T(128)} all-reduce(f32[]{:T(128)} %psum.126), channel_id=1, replica_groups=mesh['dp'=16,'tensor'=2] {'dp'}, use_global_device_ids=true, to_apply=%region_12.13 | all-reduce | flops 1 | bytes 8 | tf_op jit(solution)/shard_map/psum | solution.py:168
  600.5 39.2 %all-reduce = (f32[768]{0:T(1024)}, f32[768]{0:T(1024)}, f32[768]{0:T(1024)}, f32[3072]{0:T(1024)}, f32[768]{0:T(1024)}, /*index=5*/f32[768]{0:T(1024)}, f32[768...) all-reduce(f32[768]{0:T(1024)S(1)} %dynamic_update_slice.41, ...), channel_id=1, replica_groups=mesh['dp'=16,'tensor'=2] {'dp','tensor'}, use_global_device_ids=true, to_apply=%region_32.33 | all-reduce | flops 13070 | bytes 104560 | tf_op jit(solution)/shard_map/psum | solution.py:271
  639.6 2.5 convert_add_fusion
  642.1 73.5 %reduce-scatter.27.cloned.1.call-done = f32[96,768]{1,0:T(8,128)} async-done(((f32[1536,768]{1,0:T(8,128)}), f32[96,768]{1,0:T(8,128)}) %reduce-scatter.27.cloned.1.call-update) | async-done | bytes 294928 | tf_op jit(solution)/shard_map/reduce_scatter | solution.py:268
  715.6 61.4 %reduce-scatter.25.cloned.1.call-done = f32[24,768]{1,0:T(8,128)} async-done(((f32[384,768]{1,0:T(8,128)}), f32[24,768]{1,0:T(8,128)}) %reduce-scatter.25.cloned.1.call-update) | async-done | bytes 73744 | tf_op jit(solution)/shard_map/reduce_scatter | solution.py:267
  777.0 61.2 %reduce-scatter.23.cloned.1.call-done = f32[24,768]{1,0:T(8,128)} async-done(((f32[384,768]{1,0:T(8,128)}), f32[24,768]{1,0:T(8,128)}) %reduce-scatter.23.cloned.1.call-update) | async-done | bytes 73744 | tf_op jit(solution)/shard_map/reduce_scatter | solution.py:266
  838.2 61.0 %reduce-scatter.21.cloned.1.call-done = f32[24,768]{1,0:T(8,128)} async-done(((f32[384,768]{1,0:T(8,128)}), f32[24,768]{1,0:T(8,128)}) %reduce-scatter.21.cloned.1.call-update) | async-done | bytes 73744 | tf_op jit(solution)/shard_map/reduce_scatter | solution.py:265
  899.3 61.4 %reduce-scatter.19.cloned.1.call-done = f32[24,768]{1,0:T(8,128)} async-done(((f32[384,768]{1,0:T(8,128)}), f32[24,768]{1,0:T(8,128)}) %reduce-scatter.19.cloned.1.call-update) | async-done | bytes 73744 | tf_op jit(solution)/shard_map/reduce_scatter | solution.py:264
  (247 shorter events, 46.4 us)
Async XLA Ops:
  8.0 47.6 %copy-start.33 = (bf16[24,768]{1,0:T(8,128)(2,1)S(1)}, bf16[24,768]{1,0:T(8,128)(2,1)}, u32[]{:S(2)}) copy-start(bf16[24,768]{1,0:T(8,128)(2,1)} %param.32) | copy-start | bytes 110596
  8.0 69.3 %copy-start.34 = (bf16[24,768]{1,0:T(8,128)(2,1)S(1)}, bf16[24,768]{1,0:T(8,128)(2,1)}, u32[]{:S(2)}) copy-start(bf16[24,768]{1,0:T(8,128)(2,1)} %param.33) | copy-start | bytes 110596
  8.0 89.8 %all-gather.7.cloned.1.call-start = ((), (), s32[]{:S(2)}) async-start(), calls=%async_computation.10 | async-start | bytes 2359296 | tf_op jit(solution)/shard_map/all_gather | solution.py:112
  8.8 192.7 %reduce-scatter.11.cloned.1.call-start = ((), (), s32[]{:S(2)}) async-start(), calls=%async_computation.11 | async-start | bytes 4718592 | tf_op jit(solution)/shard_map/reduce_scatter | solution.py:148
  11.1 89.1 %copy-start.58 = (f32[6]{0:T(128)}, f32[6]{0:T(128)S(1)}, u32[]{:S(2)}) copy-start(f32[6]{0:T(128)S(1)} %dynamic_slice.58) | copy-start | bytes 76
  11.3 144.2 %copy-start.35 = (f32[384]{0:T(512)}, f32[384]{0:T(512)S(1)}, u32[]{:S(2)}) copy-start(f32[384]{0:T(512)S(1)} %mul.331) | copy-start | bytes 4612
  36.3 61.5 %copy-start.25 = (bf16[384,768]{1,0:T(8,128)(2,1)}, bf16[384,768]{1,0:T(8,128)(2,1)S(1)}, u32[]{:S(2)}) copy-start(bf16[384,768]{1,0:T(8,128)(2,1)S(1)} %all_gather.37) | copy-start | bytes 1769476
  55.6 45.6 %copy-start.29 = (bf16[384,768]{1,0:T(8,128)(2,1)}, bf16[384,768]{1,0:T(8,128)(2,1)S(1)}, u32[]{:S(2)}) copy-start(bf16[384,768]{1,0:T(8,128)(2,1)S(1)} %all_gather.38) | copy-start | bytes 1769476
  152.8 2.6 copy-start.9
  152.8 6.7 copy-start.1
  152.8 6.7 copy-start.4
  152.8 3.9 copy-start.15
  159.4 2.2 copy-start.44
  159.4 42.1 %copy-start.17 = (bf16[512,768]{1,0:T(8,128)(2,1)S(1)}, bf16[512,768]{1,0:T(8,128)(2,1)}, u32[]{:S(2)}) copy-start(bf16[512,768]{1,0:T(8,128)(2,1)} %param.27) | copy-start | bytes 2359300
  159.4 42.1 %copy-start.40 = (f32[768]{0:T(1024)S(1)}, f32[768]{0:T(1024)}, u32[]{:S(2)}) copy-start(f32[768]{0:T(1024)} %param.38) | copy-start | bytes 9220
  159.5 46.5 %all-gather.11.cloned.1.call-start = ((), (), s32[]{:S(2)}) async-start(), calls=%async_computation.13 | async-start | bytes 2506752 | tf_op jit(solution)/shard_map/all_gather | solution.py:52
  160.0 72.3 %all-gather.9.cloned.1.call-start = ((), (), s32[]{:S(2)}) async-start(), calls=%async_computation.12 | async-start | bytes 2359296 | tf_op jit(solution)/shard_map/all_gather | solution.py:154
  204.0 1.9 copy-start.56
  205.2 72.3 %all-gather.13.cloned.1.call-start = ((), (), s32[]{:S(2)}) async-start(), calls=%async_computation.14 | async-start | bytes 2506752 | tf_op jit(solution)/shard_map/all_gather | solution.py:53
  205.8 120.7 %reduce-scatter.13.cloned.1.call-start = ((), (), s32[]{:S(2)}) async-start(), calls=%async_computation.15 | async-start | bytes 4718592 | tf_op jit(solution)/shard_map/reduce_scatter | solution.py:160
  284.4 42.1 %copy-start.41 = (f32[768]{0:T(1024)S(1)}, f32[768]{0:T(1024)}, u32[]{:S(2)}) copy-start(f32[768]{0:T(1024)} %param.40) | copy-start | bytes 9220
  284.4 77.5 %all-gather.15.cloned.1.call-start = ((), (), s32[]{:S(2)}) async-start(), calls=%async_computation.16 | async-start | bytes 2359296 | tf_op jit(solution)/shard_map/all_gather | solution.py:182
  334.8 87.0 %reduce-scatter.15.cloned.1.call-start = ((), (), s32[]{:S(2)}) async-start(), calls=%async_computation.17 | async-start | bytes 4718592 | tf_op jit(solution)/shard_map/reduce_scatter | solution.py:190
  361.9 12.2 %copy-start.60 = (bf16[1536,768]{1,0:T(8,128)(2,1)S(1)}, bf16[1536,768]{1,0:T(8,128)(2,1)}, u32[]{:S(2)}) copy-start(bf16[1536,768]{1,0:T(8,128)(2,1)} %all-gather.11.cloned.1.call-done) | copy-start | bytes 7077892
  378.4 78.9 %all-gather.17.cloned.1.call-start = ((), (), s32[]{:S(2)}) async-start(), calls=%async_computation.18 | async-start | bytes 2359296 | tf_op jit(solution)/shard_map/all_gather | solution.py:199
  424.6 2.5 copy-start.14
  425.2 4.7 copy-start.10
  425.2 4.7 copy-start.37
  430.0 209.7 %reduce-scatter.17.cloned.1.call-start = ((), (), s32[]{:S(2)}) async-start(), calls=%async_computation.19 | async-start | bytes 2359296 | tf_op jit(solution)/shard_map/reduce_scatter | solution.py:257
  430.2 27.1 %copy-start.16 = (bf16[384,768]{1,0:T(8,128)(2,1)S(1)}, bf16[384,768]{1,0:T(8,128)(2,1)}, u32[]{:S(2)}) copy-start(bf16[384,768]{1,0:T(8,128)(2,1)} %all_gather.40) | copy-start | bytes 1769476
  465.0 3.4 copy-start.59
  468.5 3.1 copy-start.2
  472.3 2.9 copy-start.6
  488.0 5.9 copy-start
  488.0 5.9 copy-start.5
  496.0 2.9 copy-start.6
  512.8 5.9 copy-start
  512.8 5.9 copy-start.5
  520.4 4.1 copy-start.23
  522.6 3.0 copy-start.21
  524.5 2.4 copy-start.18
  529.2 112.9 %reduce-scatter.29.cloned.1.call-start = ((), (), s32[]{:S(2)}) async-start(), calls=%async_computation.25 | async-start | bytes 5013504 | tf_op jit(solution)/shard_map/reduce_scatter | solution.py:269
  537.3 178.3 %reduce-scatter.27.cloned.1.call-start = ((), (), s32[]{:S(2)}) async-start(), calls=%async_computation.24 | async-start | bytes 5013504 | tf_op jit(solution)/shard_map/reduce_scatter | solution.py:268
  545.4 231.6 %reduce-scatter.25.cloned.1.call-start = ((), (), s32[]{:S(2)}) async-start(), calls=%async_computation.23 | async-start | bytes 1253376 | tf_op jit(solution)/shard_map/reduce_scatter | solution.py:267
  549.2 3.7 copy-start.24
  549.2 3.7 copy-start.62
  549.2 289.0 %reduce-scatter.23.cloned.1.call-start = ((), (), s32[]{:S(2)}) async-start(), calls=%async_computation.22 | async-start | bytes 1253376 | tf_op jit(solution)/shard_map/reduce_scatter | solution.py:266
  552.9 2.3 copy-start.22
  552.9 346.4 %reduce-scatter.21.cloned.1.call-start = ((), (), s32[]{:S(2)}) async-start(), calls=%async_computation.21 | async-start | bytes 1253376 | tf_op jit(solution)/shard_map/reduce_scatter | solution.py:265
  554.8 43.8 %copy-start.54 = (f32[1536]{0:T(1024)S(1)}, f32[1536]{0:T(1024)}, u32[]{:S(2)}) copy-start(f32[1536]{0:T(1024)} %get-tuple-element.338) | copy-start | bytes 18436
  554.8 44.1 %copy-start.53 = (f32[1536]{0:T(1024)S(1)}, f32[1536]{0:T(1024)}, u32[]{:S(2)}) copy-start(f32[1536]{0:T(1024)} %get-tuple-element.363) | copy-start | bytes 18436
  554.8 44.4 %copy-start.42 = (f32[768]{0:T(1024)S(1)}, f32[768]{0:T(1024)}, u32[]{:S(2)}) copy-start(f32[768]{0:T(1024)} %get-tuple-element.277) | copy-start | bytes 9220
  554.8 44.4 %copy-start.43 = (f32[768]{0:T(1024)S(1)}, f32[768]{0:T(1024)}, u32[]{:S(2)}) copy-start(f32[768]{0:T(1024)} %get-tuple-element.286) | copy-start | bytes 9220
  554.8 44.4 %copy-start.52 = (f32[384]{0:T(512)S(1)}, f32[384]{0:T(512)}, u32[]{:S(2)}) copy-start(f32[384]{0:T(512)} %get-tuple-element.369) | copy-start | bytes 4612
  554.9 405.8 %reduce-scatter.19.cloned.1.call-start = ((), (), s32[]{:S(2)}) async-start(), calls=%async_computation.20 | async-start | bytes 1253376 | tf_op jit(solution)/shard_map/reduce_scatter | solution.py:264
  555.2 44.1 %copy-start.20 = (bf16[2,512,6,64]{1,3,2,0:T(8,128)(2,1)S(1)}, bf16[2,512,6,64]{1,3,2,0:T(8,128)(2,1)}, u32[]{:S(2)}) copy-start(bf16[2,512,6,64]{1,3,2,0:T(8,128)(2,1)} %get-tuple-element.566) | copy-start | bytes 2359300
  558.5 41.9 %copy-start.45 = (f32[768]{0:T(1024)S(1)}, f32[768]{0:T(1024)}, u32[]{:S(2)}) copy-start(f32[768]{0:T(1024)} %get-tuple-element.279) | copy-start | bytes 9220
  558.5 41.9 %copy-start.46 = (f32[768]{0:T(1024)S(1)}, f32[768]{0:T(1024)}, u32[]{:S(2)}) copy-start(f32[768]{0:T(1024)} %get-tuple-element.283) | copy-start | bytes 9220
  558.5 41.9 %copy-start.47 = (f32[768]{0:T(1024)S(1)}, f32[768]{0:T(1024)}, u32[]{:S(2)}) copy-start(f32[768]{0:T(1024)} %get-tuple-element.336) | copy-start | bytes 9220
  558.5 41.9 %copy-start.48 = (f32[768]{0:T(1024)S(1)}, f32[768]{0:T(1024)}, u32[]{:S(2)}) copy-start(f32[768]{0:T(1024)} %get-tuple-element.364) | copy-start | bytes 9220
  558.5 41.9 %copy-start.50 = (f32[768]{0:T(1024)S(1)}, f32[768]{0:T(1024)}, u32[]{:S(2)}) copy-start(f32[768]{0:T(1024)} %get-tuple-element.281) | copy-start | bytes 9220
  558.5 41.9 %copy-start.51 = (f32[768]{0:T(1024)S(1)}, f32[768]{0:T(1024)}, u32[]{:S(2)}) copy-start(f32[768]{0:T(1024)} %get-tuple-element.285) | copy-start | bytes 9220
  558.5 81.1 %copy-start.11 = (f32[512,768]{1,0:T(8,128)S(1)}, f32[512,768]{1,0:T(8,128)}, u32[]{:S(2)}) copy-start(f32[512,768]{1,0:T(8,128)} %copy-done.10) | copy-start | bytes 4718596
  558.5 81.1 %copy-start.38 = (f32[512]{0:T(512)S(1)}, f32[512]{0:T(512)}, u32[]{:S(2)}) copy-start(f32[512]{0:T(512)} %copy-done.37) | copy-start | bytes 6148
  (22 other events, 29.9 us)
Sparse Core Ops, SparseCore 0:
  10.4 29.9 all-gather.6
  159.6 41.9 reduce-scatter.10
  284.5 41.8 reduce-scatter.12
  430.1 27.2 all-gather.16
  529.3 26.0 reduce-scatter.16
  559.7 76.1 reduce-scatter.28
  640.8 74.7 reduce-scatter.26
  719.8 57.1 reduce-scatter.24
  781.2 56.9 reduce-scatter.22
  842.3 56.9 reduce-scatter.20
  903.5 57.1 reduce-scatter.18
Sparse Core Ops, SparseCore 1:
  162.5 41.1 all-gather.10
  205.7 26.6 all-gather.8
  234.8 42.7 all-gather.12
  334.9 27.0 all-gather.14
  378.5 43.2 reduce-scatter.14
